TPU v7x, 256 devices: a whole 4x4x8 slice. The times are simulated.
256 devices in a mesh: expert: 64 (over z, x, core), mp: 4 (over y).
Axes of the slice: x: 4, y: 4, z: 8, core: 2. Of those that a mesh axis runs over, the one named last changes fastest.
Arguments:
- tokens: bfloat16 [16384, 1024], P('expert'), may hold values from -6 to 6
- cotangent: bfloat16 [16384, 1024], P('expert'), may hold values from -16 to 16
- routes: int32 [16384, 2], P('expert'), may hold values from 0 to 63, all different within a row; in each aligned block of 256 rows (0 to 255, 256 to 511, ...) at most 12 rows name the same one
- router_weight: bfloat16 [1024, 64], replicated, may hold values from -0.1875 to 0.1875
- gate_weight: bfloat16 [64, 1024, 3584], P('expert', None, 'mp'), may hold values from -0.1875 to 0.1875
- up_weight: bfloat16 [64, 1024, 3584], P('expert', None, 'mp'), may hold values from -0.6875 to 0.6875
- down_weight: bfloat16 [64, 3584, 1024], P('expert', 'mp'), may hold values from -0.3674842 to 0.3674842
- mlp_in: float32 [3, 16], replicated, may hold values from -3.5 to 3.5
- mlp_bias: float32 [16], replicated, may hold values from -2 to 2
- mlp_out: float32 [16], replicated, may hold values from -1.5 to 1.5
Outputs:
- mixed: bfloat16 [16384, 1024], P('expert', 'mp')
- gate_update: bfloat16 [64, 1024, 3584], P('expert', None, 'mp')
- up_update: bfloat16 [64, 1024, 3584], P('expert', None, 'mp')
- down_update: bfloat16 [64, 3584, 1024], P('expert', 'mp')
- router_update: bfloat16 [1024, 64], replicated
Inputs may be any that keep to these rules, and one draw needn't show every extreme that they name: `routes`: in the rows of one index of the expert axis each expert is named at most 12 times; the two experts of a row differ.
All inputs are finite; a program needn't handle non-finite values.
Results may differ from a plain program's by a relative error of at most 0.0057.
Values may be sent and summed in bfloat16 or wider, within the bound.
No kernel may reach another device: no remote copies, remote signals or barrier semaphores. Data moves between devices by JAX's collectives and lax.ppermute only.
A program may use at most 128 MiB of HBM per device.

v0:
```python
import functools

import jax
import jax.numpy as jnp
from jax import lax
from jax.sharding import Mesh
from jax.sharding import PartitionSpec as P

D = 1024
FF = 3584
EXPERT = ("expert_0", "expert_1", "expert_2")
EXPERT_MP = ("expert_0", "expert_1", "expert_2", "mp")


EPSILON = 1e-06


def sent_together(arrays, axis, split_dim, concat_dim, along):
    both = jnp.concatenate(arrays, axis=along)
    whole, at, outs = (
        lax.all_to_all(both, axis, split_axis=split_dim, concat_axis=concat_dim, tiled=True),
        0,
        [],
    )
    for a in arrays:
        outs.append(lax.slice_in_dim(whole, at, at + a.shape[along], axis=along))
        at += a.shape[along]
    return tuple(outs)


def copy_for_each(x, axis):
    length = lax.axis_size(axis)
    return lax.all_to_all(jnp.broadcast_to(x[None], (length, *x.shape)), axis, 0, 0, tiled=True)


def of_everyone(x, axis):
    everything = copy_for_each(x, axis)
    return jnp.sum(everything, axis=0)


def by_axis(x, axes):
    return functools.reduce(lax.psum, axes, x)


def learned_step(gradient, weight, weight_scale, grad_rms, mlp_in, mlp_bias, mlp_out):
    feat_grad = gradient / grad_rms
    feat_weight = weight.astype(jnp.float32) * weight_scale
    feat_tanh = jnp.tanh(feat_grad)
    summed = jnp.zeros_like(feat_grad)
    for neuron in range(mlp_bias.shape[0]):
        hidden = jnp.maximum(
            mlp_in[0, neuron] * feat_grad
            + mlp_in[1, neuron] * feat_weight
            + mlp_in[2, neuron] * feat_tanh
            + mlp_bias[neuron],
            0.0,
        )
        summed = summed + mlp_out[neuron] * hidden
    return summed.astype(jnp.bfloat16)


def route_tables(routes, experts, capacity):
    chosen = (routes[:, :, None] == jnp.arange(experts, dtype=jnp.int32)[None, None, :]).astype(
        jnp.int32
    )
    flat_picks = chosen.reshape(-1, experts)
    before = jnp.cumsum(flat_picks, axis=0) - flat_picks
    places = jnp.sum(before * flat_picks, axis=1).reshape(routes.shape)
    slot_hit = (places[:, :, None] == jnp.arange(capacity, dtype=jnp.int32)[None, None, :]).astype(
        jnp.bfloat16
    )
    mover = chosen.astype(jnp.bfloat16)[:, :, :, None] * slot_hit[:, :, None, :]
    return (chosen.astype(jnp.float32), mover)


def on_device(
    tokens,
    cotangent,
    routes,
    router_weight,
    gate_weight,
    up_weight,
    down_weight,
    mlp_in,
    mlp_bias,
    mlp_out,
):
    experts = lax.axis_size(EXPERT)
    groups = lax.axis_size("mp")
    tok_count = tokens.shape[0]
    capacity = 3 * tok_count // experts
    width = tokens.shape[1]
    col_width = width // groups
    col_start = lax.axis_index("mp") * col_width
    chosen, mover = route_tables(routes, experts, capacity)
    logits = jnp.dot(tokens, router_weight, preferred_element_type=jnp.float32)
    picked = jnp.sum(logits[:, None, :] * chosen, axis=2)
    sigmas = jax.nn.sigmoid(picked)
    denominator = jnp.sum(sigmas, axis=1, keepdims=True)
    gates = sigmas / denominator
    scaled_cot = (gates[:, :, None] * cotangent.astype(jnp.float32)[:, None, :]).astype(
        jnp.bfloat16
    )
    token_cols = lax.dynamic_slice_in_dim(tokens, col_start, col_width, 1)
    cot_cols = lax.dynamic_slice_in_dim(cotangent, col_start, col_width, 1)
    send_x = jnp.einsum("tkec,td->ecd", mover, tokens, preferred_element_type=jnp.float32).astype(
        jnp.bfloat16
    )
    send_dy = jnp.einsum(
        "tkec,tkd->ecd", mover, scaled_cot, preferred_element_type=jnp.float32
    ).astype(jnp.bfloat16)
    rows_x, rows_dy = sent_together((send_x, send_dy), EXPERT, 0, 0, 1)
    rows_x = rows_x.reshape(experts * capacity, width)
    rows_dy = rows_dy.reshape(experts * capacity, width)
    w_gate = gate_weight[0]
    w_up = up_weight[0]
    w_down = down_weight[0]
    act_gate = jnp.dot(rows_x, w_gate, preferred_element_type=jnp.float32)
    act_up = jnp.dot(rows_x, w_up, preferred_element_type=jnp.float32)
    sigmoid_gate = jax.nn.sigmoid(act_gate)
    silu_gate = act_gate * sigmoid_gate
    hidden = (silu_gate * act_up).astype(jnp.bfloat16)
    partial_out = jnp.dot(hidden, w_down, preferred_element_type=jnp.float32)
    expert_sums = lax.psum_scatter(partial_out, "mp", scatter_dimension=1, tiled=True)
    back_rows = expert_sums.astype(jnp.bfloat16).reshape(experts, capacity, col_width)
    returned = lax.all_to_all(back_rows, EXPERT, split_axis=0, concat_axis=0, tiled=True)
    grad_down = jnp.einsum("sf,sd->fd", hidden, rows_dy, preferred_element_type=jnp.float32)
    grad_hidden = jnp.einsum("sd,fd->sf", rows_dy, w_down, preferred_element_type=jnp.float32)
    d_gate = (grad_hidden * act_up * sigmoid_gate * (1.0 + act_gate * (1.0 - sigmoid_gate))).astype(
        jnp.bfloat16
    )
    d_up = (grad_hidden * silu_gate).astype(jnp.bfloat16)
    grad_gate = jnp.einsum("sd,sf->df", rows_x, d_gate, preferred_element_type=jnp.float32)
    grad_up = jnp.einsum("sd,sf->df", rows_x, d_up, preferred_element_type=jnp.float32)
    routed = jnp.einsum("tkec,ecd->tkd", mover, returned, preferred_element_type=jnp.float32)
    mixed = (
        token_cols.astype(jnp.float32) + gates[:, 0:1] * routed[:, 0] + gates[:, 1:2] * routed[:, 1]
    ).astype(jnp.bfloat16)
    partial_dots = jnp.sum(cot_cols.astype(jnp.float32)[:, None, :] * routed, axis=2)
    gate_grads = of_everyone(partial_dots, "mp")
    mean_part = jnp.sum(gates * gate_grads, axis=1, keepdims=True)
    sigma_grads = (gate_grads - mean_part) / denominator
    logit_grads = sigma_grads * sigmas * (1.0 - sigmas)
    dense_grads = jnp.sum(logit_grads[:, :, None] * chosen, axis=1).astype(jnp.bfloat16)
    router_part = jnp.einsum("td,te->de", tokens, dense_grads, preferred_element_type=jnp.float32)
    norm_sums = (
        by_axis(jnp.sum(grad_gate * grad_gate), EXPERT_MP),
        by_axis(jnp.sum(grad_up * grad_up), EXPERT_MP),
        by_axis(jnp.sum(grad_down * grad_down), EXPERT_MP),
    )
    total_count = experts * width * w_gate.shape[1] * groups
    gate_rms = jnp.sqrt(norm_sums[0] / total_count + EPSILON)
    up_rms = jnp.sqrt(norm_sums[1] / total_count + EPSILON)
    down_rms = jnp.sqrt(norm_sums[2] / total_count + EPSILON)
    gate_update = learned_step(grad_gate, w_gate, D**0.5, gate_rms, mlp_in, mlp_bias, mlp_out)[None]
    up_update = learned_step(grad_up, w_up, D**0.5, up_rms, mlp_in, mlp_bias, mlp_out)[None]
    down_update = learned_step(grad_down, w_down, FF**0.5, down_rms, mlp_in, mlp_bias, mlp_out)[
        None
    ]
    router_count = width * experts
    router_grad = by_axis(router_part, EXPERT)
    router_rms = jnp.sqrt(jnp.sum(router_grad * router_grad) / router_count + EPSILON)
    router_update = learned_step(
        router_grad, router_weight, D**0.5, router_rms, mlp_in, mlp_bias, mlp_out
    )
    return (mixed, gate_update, up_update, down_update, router_update)


def solution(mesh):
    torus = Mesh(
        mesh.devices.reshape(8, 4, 2, mesh.shape["mp"]), ("expert_0", "expert_1", "expert_2", "mp")
    )
    placed = (
        P(EXPERT, None),
        P(EXPERT, None),
        P(EXPERT, None),
        P(),
        P(EXPERT, None, "mp"),
        P(EXPERT, None, "mp"),
        P(EXPERT, "mp", None),
        P(),
        P(),
        P(),
    )
    return jax.shard_map(
        on_device,
        mesh=torus,
        in_specs=placed,
        out_specs=(
            P(EXPERT, "mp"),
            P(EXPERT, None, "mp"),
            P(EXPERT, None, "mp"),
            P(EXPERT, "mp", None),
            P(),
        ),
        check_vma=False,
    )
```

profile of v0, /device:TPU:1, one launch (start us, length us, event | category | flops | bytes accessed | tf_op | source)
XLA Modules:
  0.0 483.5 jit_solution(582187653571179689)
XLA Ops:
  9.1 1.2 convert_element_type.103
  10.3 1.2 fusion.442
  13.4 1.2 reduce-window.6
  17.4 1.7 copy.36
  19.1 85.6 %all_to_all.15 = bf16[64,24,1024]{2,1,0:T(8,128)(2,1)S(1)} all-to-all(bf16[64,24,1024]{2,1,0:T(8,128)(2,1)S(1)} %copy.36), channel_id=1, replica_groups=mesh['expert_0'=8,'expert_1'=4,'expert_2'=2,'mp'=4] {'expert_0','expert_..., dimensions={0} | all-to-all | bytes 6291456 | tf_op jit(solution)/shard_map/all_to_all | solution.py:21
  104.7 2.5 fusion.435
  107.2 3.6 reshape.174
  110.8 3.9 fusion.295
  114.8 3.4 multiply_convert_fusion.2
  118.2 1.1 copy-done.23
  119.3 3.5 fusion.291
  148.7 1.3 reshape.176
  150.1 4.0 fusion.289
  154.1 1.5 copy-done.24
  155.6 4.8 multiply_reduce_fusion.2
  161.2 1.2 convert_element_type.107
  163.3 10.6 %all-to-all-start.1 = ((bf16[64,12,256]{2,1,0:T(8,128)(2,1)}), bf16[64,12,256]{2,1,0:T(8,128)(2,1)S(1)}, u32[]{:S(2)}, u32[]{:S(2)}) async-start(bf16[64,12,256]{2,1,0:T(8,128)(2,1)} %reshape.175), calls=%async_computation.2 | async-start | bytes 1048576 | tf_op jit(solution)/shard_map/all_to_all | solution.py:126
  173.9 7.2 %multiply_reduce_fusion.1 = (f32[]{:T(128)}, f32[1024,896]{1,0:T(8,128)}) fusion(bf16[768,1024]{1,0:T(8,128)(2,1)S(1)} %copy-done.6, f32[768,896]{1,0:T(8,128)} %copy-done.24, f32[768,896]{1,0:T(8,128)} %copy-done.21), kind=kOutput, calls=%fused_computation.350 | convolution fusion | flops 1415249920 | bytes 10747908 | tf_op jit(solution)/shard_map/sd,sf->df/dot_general | solution.py:134
  181.1 10.5 %all-to-all-done.1 = bf16[64,12,256]{2,1,0:T(8,128)(2,1)S(1)} async-done(((bf16[64,12,256]{2,1,0:T(8,128)(2,1)}), bf16[64,12,256]{2,1,0:T(8,128)(2,1)S(1)}, u32[]{:S(2)}, u32[]{:S(2)}) %all-to-all-start.1) | async-done | bytes 393248 | tf_op jit(solution)/shard_map/all_to_all | solution.py:126
  191.6 1.3 multiply_reduce_fusion.3
  193.5 3.2 all-to-all-start.2
  196.8 6.0 %multiply_reduce_fusion = (f32[]{:T(128)}, f32[896,1024]{1,0:T(8,128)}) fusion(bf16[768,896]{1,0:T(8,128)(2,1)} %copy-done.23, bf16[768,1024]{1,0:T(8,128)(2,1)} %reshape.176), kind=kOutput, calls=%fused_computation.341 | convolution fusion | flops 1411121152 | bytes 6619140 | tf_op jit(solution)/shard_map/sf,sd->fd/dot_general | solution.py:127
  202.8 13.2 %all-reduce = (f32[]{:T(128)}, f32[]{:T(128)}, f32[]{:T(128)}) all-reduce(f32[]{:T(128)} %get-tuple-element.120, f32[]{:T(128)} %get-tuple-element.122, f32[]{:T(128)} %get-tuple-element.124), channel_id=1, replica_groups=mesh['expert_0'=8,'expert_1'=4,'expert_2'=2,'mp'=4] {'expert_0'}, use_global_device_ids=true, to_apply=%region_8.9 | all-reduce | flops 3 | bytes 24 | tf_op jit(solution)/shard_map/psum | solution.py:42
  216.0 7.3 %all-reduce.2 = (f32[]{:T(128)}, f32[]{:T(128)}, f32[]{:T(128)}) all-reduce(f32[]{:T(128)} %get-tuple-element.20, f32[]{:T(128)} %get-tuple-element.21, f32[]{:T(128)} %get-tuple-element.22), channel_id=1, replica_groups=mesh['expert_0'=8,'expert_1'=4,'expert_2'=2,'mp'=4] {'expert_1'}, use_global_device_ids=true, to_apply=%region_9.10 | all-reduce | flops 3 | bytes 24 | tf_op jit(solution)/shard_map/psum | solution.py:42
  223.3 9.2 %all-reduce.3 = (f32[]{:T(128)}, f32[]{:T(128)}, f32[]{:T(128)}) all-reduce(f32[]{:T(128)} %get-tuple-element.26, f32[]{:T(128)} %get-tuple-element.27, f32[]{:T(128)} %get-tuple-element.28), channel_id=1, replica_groups=mesh['expert_0'=8,'expert_1'=4,'expert_2'=2,'mp'=4] {'expert_2'}, use_global_device_ids=true, to_apply=%region_10.11 | all-reduce | flops 3 | bytes 24 | tf_op jit(solution)/shard_map/psum | solution.py:42
  232.5 9.6 %all-reduce.1 = (f32[]{:T(128)}, f32[]{:T(128)}, f32[]{:T(128)}) all-reduce(f32[]{:T(128)} %get-tuple-element.29, f32[]{:T(128)} %get-tuple-element.30, f32[]{:T(128)} %get-tuple-element.31), channel_id=1, replica_groups=mesh['expert_0'=8,'expert_1'=4,'expert_2'=2,'mp'=4] {'mp'}, use_global_device_ids=true, to_apply=%region_11.12 | all-reduce | flops 3 | bytes 24 | tf_op jit(solution)/shard_map/psum | solution.py:42
  243.9 60.5 %fusion.297 = bf16[1,1024,896]{2,1,0:T(8,128)(2,1)} fusion(f32[]{:T(128)} %bitcast.94, f32[]{:T(128)} %bitcast.93, f32[]{:T(128)} %bitcast.92, f32[]{:T(128)} %bitcast.91, f32[]{:T(128)} %bitcast.90, f32[]{:T(128)} %bitcast.89, f32[]{:T(128)} %bitcast.88, f32[]{:T(128)} %bitcast.87, f32[]{:T(128)} %bitcast.86, f32[]{:T(128)} %bitcast.85, f32[]{:T(128)} %bitcast.84, ...), kind=kLoop, calls=%fused_computation.379 | loop fusion | flops 133955584 | bytes 7340356 | tf_op jit(solution)/shard_map/broadcast_in_dim | solution.py:155
  305.2 3.1 all-reduce.8.cloned.1.call-done
  308.6 61.1 %fusion.298 = bf16[1,1024,896]{2,1,0:T(8,128)(2,1)} fusion(f32[]{:T(128)} %bitcast.94, f32[]{:T(128)} %bitcast.93, f32[]{:T(128)} %bitcast.92, f32[]{:T(128)} %bitcast.91, f32[]{:T(128)} %bitcast.90, f32[]{:T(128)} %bitcast.89, f32[]{:T(128)} %bitcast.88, f32[]{:T(128)} %bitcast.87, f32[]{:T(128)} %bitcast.86, f32[]{:T(128)} %bitcast.85, f32[]{:T(128)} %bitcast.84, ...), kind=kLoop, calls=%fused_computation.380 | loop fusion | flops 133955584 | bytes 7340356 | tf_op jit(solution)/shard_map/broadcast_in_dim | solution.py:156
  370.5 60.4 %fusion.299 = bf16[1,896,1024]{2,1,0:T(8,128)(2,1)} fusion(f32[]{:T(128)} %bitcast.94, f32[]{:T(128)} %bitcast.93, f32[]{:T(128)} %bitcast.112, f32[]{:T(128)} %bitcast.91, f32[]{:T(128)} %bitcast.90, f32[]{:T(128)} %bitcast.89, f32[]{:T(128)} %bitcast.88, f32[]{:T(128)} %bitcast.111, f32[]{:T(128)} %bitcast.86, f32[]{:T(128)} %bitcast.85, f32[]{:T(128)} %bitcast.84, ...), kind=kLoop, calls=%fused_computation.381 | loop fusion | flops 133955584 | bytes 7340356 | tf_op jit(solution)/shard_map/broadcast_in_dim | solution.py:157
  431.7 1.6 multiply_reduce_fusion.4
  434.0 43.0 %fusion.420 = bf16[1024,64]{0,1:T(8,128)(2,1)} fusion(bf16[1024,64]{0,1:T(8,128)(2,1)S(1)} %copy-done.7, f32[1024,64]{0,1:T(8,128)} %all-reduce.12.cloned.1.call-done, f32[]{:T(128)} %bitcast.94, f32[]{:T(128)} %bitcast.93, f32[]{:T(128)} %bitcast.92, f32[]{:T(128)} %bitcast.91, f32[]{:T(128)} %bitcast.90, f32[]{:T(128)} %bitcast.89, f32[]{:T(128)} %bitcast.88, ...), kind=kLoop, calls=%fused_computation.529 | loop fusion | flops 9568256 | bytes 524612 | tf_op jit(solution)/shard_map/convert_element_type | solution.py:59
  (100 shorter events, 17.2 us)
Async XLA Ops:
  7.2 3.1 copy-start
  7.2 154.0 %reduce-scatter.2.cloned.1.call-start = ((), (), s32[]{:S(2)}) async-start(), calls=%async_computation.4 | async-start | bytes 3932160 | tf_op jit(solution)/shard_map/reduce_scatter | solution.py:124
  9.1 8.0 %copy-start.10 = (bf16[256,2,64]{0,2,1:T(8,128)(2,1)}, bf16[256,2,64]{0,2,1:T(8,128)(2,1)S(1)}, u32[]{:S(2)}) copy-start(bf16[256,2,64]{0,2,1:T(8,128)(2,1)S(1)} %convert_convert_fusion) | copy-start | bytes 196612
  12.2 0.6 copy-start.14
  12.8 0.6 copy-start.16
  110.8 3.9 copy-start.2
  110.8 3.9 copy-start.5
  114.7 3.5 copy-start.21
  114.8 4.5 copy-start.3
  118.2 1.1 copy-start.23
  119.3 3.5 copy-start.8
  122.8 24.0 %copy-start.11 = (f32[16]{0:T(128)S(1)}, f32[16]{0:T(128)}, u32[]{:S(2)}) copy-start(f32[16]{0:T(128)} %param.18) | copy-start | bytes 196
  122.8 24.7 %copy-start.12 = (f32[16]{0:T(128)S(1)}, f32[16]{0:T(128)}, u32[]{:S(2)}) copy-start(f32[16]{0:T(128)} %param.19) | copy-start | bytes 196
  150.1 5.5 %copy-start.6 = (bf16[768,1024]{1,0:T(8,128)(2,1)S(1)}, bf16[768,1024]{1,0:T(8,128)(2,1)}, u32[]{:S(2)}) copy-start(bf16[768,1024]{1,0:T(8,128)(2,1)} %reshape.174) | copy-start | bytes 4718596
  150.1 5.5 %copy-start.22 = (f32[768,896]{1,0:T(8,128)S(1)}, f32[768,896]{1,0:T(8,128)}, u32[]{:S(2)}) copy-start(f32[768,896]{1,0:T(8,128)} %copy-done.21) | copy-start | bytes 8257540
  150.1 5.5 %copy-start.25 = (f32[768,896]{1,0:T(8,128)S(1)}, f32[768,896]{1,0:T(8,128)}, u32[]{:S(2)}) copy-start(f32[768,896]{1,0:T(8,128)} %get-tuple-element.119) | copy-start | bytes 8257540
  154.1 1.5 copy-start.24
  163.3 28.3 %all-to-all-start.1 = ((bf16[64,12,256]{2,1,0:T(8,128)(2,1)}), bf16[64,12,256]{2,1,0:T(8,128)(2,1)S(1)}, u32[]{:S(2)}, u32[]{:S(2)}) async-start(bf16[64,12,256]{2,1,0:T(8,128)(2,1)} %reshape.175), calls=%async_computation.2 | async-start | bytes 1048576 | tf_op jit(solution)/shard_map/all_to_all | solution.py:126
  173.9 17.7 %copy-start.9 = (f32[256,256]{0,1:T(8,128)S(1)}, f32[256,256]{0,1:T(8,128)}, u32[]{:S(2)}) copy-start(f32[256,256]{0,1:T(8,128)} %copy.38) | copy-start | bytes 786436
  193.5 49.3 %all-to-all-start.2 = ((f32[4,256,2]{1,2,0:T(2,128)}), f32[4,256,2]{1,2,0:T(2,128)S(1)}, u32[]{:S(2)}, u32[]{:S(2)}) async-start(f32[4,256,2]{1,2,0:T(2,128)} %broadcast_in_dim.11), calls=%async_computation.3 | async-start | bytes 16384 | tf_op jit(solution)/shard_map/all_to_all | solution.py:33
  196.7 46.1 %copy-start.15 = (f32[256,2]{0,1:T(2,128)S(1)}, f32[256,2]{0,1:T(2,128)}, u32[]{:S(2)}) copy-start(f32[256,2]{0,1:T(2,128)} %copy-done.14) | copy-start | bytes 6148
  196.7 46.1 %copy-start.17 = (f32[256]{0:T(256)S(1)}, f32[256]{0:T(256)}, u32[]{:S(2)}) copy-start(f32[256]{0:T(256)} %copy-done.16) | copy-start | bytes 3076
  196.8 46.1 %copy-start.18 = (f32[256,2]{0,1:T(2,128)S(1)}, f32[256,2]{0,1:T(2,128)}, u32[]{:S(2)}) copy-start(f32[256,2]{0,1:T(2,128)} %get-tuple-element.33) | copy-start | bytes 6148
  196.8 46.1 %copy-start.13 = (s32[256,2]{0,1:T(2,128)S(1)}, s32[256,2]{0,1:T(2,128)}, u32[]{:S(2)}) copy-start(s32[256,2]{0,1:T(2,128)} %param.12) | copy-start | bytes 6148
  196.8 47.1 %copy-start.1 = (bf16[1,1024,896]{2,1,0:T(8,128)(2,1)S(1)}, bf16[1,1024,896]{2,1,0:T(8,128)(2,1)}, u32[]{:S(2)}) copy-start(bf16[1,1024,896]{2,1,0:T(8,128)(2,1)} %param.14) | copy-start | bytes 5505028
  196.8 111.5 %all-reduce.8.cloned.1.call-start = ((), (), s32[]{:S(2)}) async-start(), calls=%async_computation.5 | async-start | bytes 524288 | tf_op jit(solution)/shard_map/psum | solution.py:42
  243.9 126.5 %all-reduce.10.cloned.1.call-start = ((), (), s32[]{:S(2)}) async-start(), calls=%async_computation.6 | async-start | bytes 524288 | tf_op jit(solution)/shard_map/psum | solution.py:42
  308.3 123.4 %all-reduce.12.cloned.1.call-start = ((), (), s32[]{:S(2)}) async-start(), calls=%async_computation.7 | async-start | bytes 524288 | tf_op jit(solution)/shard_map/psum | solution.py:42
  308.6 61.9 %copy-start.4 = (bf16[1,896,1024]{2,1,0:T(8,128)(2,1)S(1)}, bf16[1,896,1024]{2,1,0:T(8,128)(2,1)}, u32[]{:S(2)}) copy-start(bf16[1,896,1024]{2,1,0:T(8,128)(2,1)} %param.16) | copy-start | bytes 5505028
  370.4 60.5 %copy-start.19 = (f32[256,1]{0,1:T(1,128)S(1)}, f32[256,1]{0,1:T(1,128)}, u32[]{:S(2)}) copy-start(f32[256,1]{0,1:T(1,128)} %get-tuple-element.84) | copy-start | bytes 3076
  370.4 60.5 %copy-start.20 = (f32[256,1]{0,1:T(1,128)S(1)}, f32[256,1]{0,1:T(1,128)}, u32[]{:S(2)}) copy-start(f32[256,1]{0,1:T(1,128)} %get-tuple-element.85) | copy-start | bytes 3076
  370.4 63.6 %copy-start.7 = (bf16[1024,64]{0,1:T(8,128)(2,1)S(1)}, bf16[1024,64]{0,1:T(8,128)(2,1)}, u32[]{:S(2)}) copy-start(bf16[1024,64]{0,1:T(8,128)(2,1)} %param.13) | copy-start | bytes 393220
Sparse Core Ops, SparseCore 0:
  122.9 38.2 reduce-scatter.1
  244.0 64.2 all-reduce.7
  310.7 47.5 all-reduce.9
  370.5 32.6 all-reduce.11
where the time goes:
time: 491 us; the launch traced here: 484 us
  other arithmetic  234 us (48%)
  blocking collectives  125 us (25%)
  matrix products  37.7 us (8%)
  between operations  36.9 us (8%)
  local copies, waits for them, and re-layouts  21.4 us (4%)
  waiting for transfers between devices  14.5 us (3%)
  starting transfers between devices  14.3 us (3%)
    all_to_all x1, blocking collectives, sent_together(): lax.all_to_all(both, axis, split_axis=split_dim, concat_axis=concat_dim,...  85.6 us
    broadcast_in_dim x1, other arithmetic, on_device(): learned_step(grad_up, w_up, D ** 0.5, up_rms, mlp_in, mlp_bias, mlp_out)  61.1 us
    broadcast_in_dim x1, other arithmetic, on_device(): learned_step(grad_gate, w_gate, D ** 0.5, gate_rms, mlp_in, mlp_bias, mlp...  60.5 us
    broadcast_in_dim x1, other arithmetic, on_device(): learned_step(grad_down, w_down, FF ** 0.5, down_rms, mlp_in, mlp_bias, ml...  60.4 us
    convert_element_type x1, other arithmetic, learned_step(): return summed.astype(jnp.bfloat16)  43 us
    psum x4, blocking collectives, by_axis(): return functools.reduce(lax.psum, axes, x)  39.3 us
    all_to_all x1, starting transfers between devices, on_device(): lax.all_to_all(back_rows, EXPERT, split_axis=0, concat_axis=0, tiled=True)  10.6 us
    all_to_all x1, waiting for transfers between devices, on_device(): lax.all_to_all(back_rows, EXPERT, split_axis=0, concat_axis=0, tiled=True)  10.5 us
  transfers between devices with their start and end apart: 6, of which 3 were waited for; matrix products, arithmetic and copies ran while one was open for 44% of the time, Pallas kernels for 0%

commit v1 on v0

v1 whole, which is shorter than its diff:
```python
import functools

import jax
import jax.numpy as jnp
from jax import lax
from jax.experimental import pallas as pl
from jax.experimental.pallas import tpu as pltpu
from jax.sharding import Mesh
from jax.sharding import PartitionSpec as P

D = 1024
FF = 3584
UNITS = 16
EXPERT = ("expert_0", "expert_1", "expert_2")
EXPERT_MP = ("expert_0", "expert_1", "expert_2", "mp")
MP_EXPERT = ("mp", "expert_0", "expert_1", "expert_2")
EPSILON = 1e-06

CAP = 12
GROUP = 16
BLOCK = GROUP * CAP
LANES = 128
BF = jnp.bfloat16
F32 = jnp.float32
HIGHEST = lax.Precision.HIGHEST


def params(**kw):
    return pltpu.CompilerParams(vmem_limit_bytes=48 << 20, **kw)


def iota(shape, dim):
    return lax.broadcasted_iota(jnp.int32, shape, dim)


def dot(a, b, dims=((1,), (0,)), **kw):
    return lax.dot_general(a, b, (dims, ((), ())), preferred_element_type=F32, **kw)


def row_sum(x):
    return jnp.sum(x, axis=1, keepdims=True)


def send_kernel(mp, tok, tok_cols, cot_cols, routes, router, x_out, dy_out, aux_out):
    del mp
    n = tok.shape[0]
    experts = router.shape[1]
    rows = experts * 2 * CAP
    lane_e = iota((n, experts), 1)
    ids = [routes[:, k : k + 1] for k in range(2)]
    hits = [(ids[k] == lane_e).astype(F32) for k in range(2)]
    earlier = (iota((n, n), 0) > iota((n, n), 1)).astype(F32).astype(BF)
    before = dot(earlier, (hits[0] + hits[1]).astype(BF))
    places = [row_sum(before * hits[k]) for k in range(2)]
    base = [ids[k] * (2 * CAP) + places[k].astype(jnp.int32) for k in range(2)]
    lane_r = iota((n, rows), 1)
    picks = [
        [(base[k] + h * CAP == lane_r).astype(F32).astype(BF) for h in range(2)] for k in range(2)
    ]
    total = jnp.zeros((rows, LANES), F32)
    for h in range(2):
        total = total + dot(
            picks[0][h] + picks[1][h], tok_cols[:, h * LANES : (h + 1) * LANES], ((0,), (0,))
        )
    x_out[...] = total.astype(BF)
    logits = dot(tok[...], router[...])
    sig = [1.0 / (1.0 + jnp.exp(-row_sum(logits * hits[k]))) for k in range(2)]
    denominator = sig[0] + sig[1]
    gates = [s / denominator for s in sig]
    cot = cot_cols[...].astype(F32)
    total = jnp.zeros((rows, LANES), F32)
    for k in range(2):
        scaled = (gates[k] * cot).astype(BF)
        for h in range(2):
            total = total + dot(picks[k][h], scaled[:, h * LANES : (h + 1) * LANES], ((0,), (0,)))
    dy_out[...] = total.astype(BF)
    lane = iota((n, LANES), 1)
    aux = jnp.zeros((n, LANES), F32)
    columns = gates + sig + [i.astype(F32) for i in ids] + places
    for i, column in enumerate(columns):
        aux = jnp.where(lane == i, column, aux)
    aux_out[...] = aux


def send_rows(tokens, cotangent, routes, router_weight, mp_index):
    n, width = tokens.shape
    experts = router_weight.shape[1]
    cols = 2 * LANES
    rows = experts * 2 * CAP
    whole = lambda *shape: pl.BlockSpec(shape, lambda i, mp: (0,) * len(shape))
    mine = pl.BlockSpec((n, cols), lambda i, mp: (0, mp[0]))
    return pl.pallas_call(
        send_kernel,
        grid_spec=pltpu.PrefetchScalarGridSpec(
            num_scalar_prefetch=1,
            grid=(1,),
            in_specs=[whole(n, width), mine, mine, whole(n, 2), whole(width, experts)],
            out_specs=[whole(rows, LANES), whole(rows, LANES), whole(n, LANES)],
        ),
        out_shape=[
            jax.ShapeDtypeStruct((rows, LANES), BF),
            jax.ShapeDtypeStruct((rows, LANES), BF),
            jax.ShapeDtypeStruct((n, LANES), F32),
        ],
        compiler_params=params(),
        name="send_rows",
    )(mp_index, tokens, tokens, cotangent, routes, router_weight)


def unpack_rows(perm, messages, at, to, blocks):
    groups = messages.shape[0]
    for b in range(blocks):
        piece = jnp.concatenate(
            [messages[m, (at + b) * 2 * BLOCK : (at + b + 1) * 2 * BLOCK, :] for m in range(groups)],
            axis=1,
        )
        both = dot(perm, piece).astype(BF)
        for h in range(2):
            for m in range(groups):
                c = (2 * m + h) * LANES
                to[b * BLOCK : (b + 1) * BLOCK, c : c + LANES] = both[
                    h * BLOCK : (h + 1) * BLOCK, m * LANES : (m + 1) * LANES
                ]


def forward_kernel(perm, perm_t, msg, gate, up, down, rows_x, hidden, by_gate, by_up, parts):
    step = pl.program_id(0)

    @pl.when(step == 0)
    def _():
        unpack_rows(perm[...], msg, 0, rows_x, rows_x.shape[0] // BLOCK)

    acts = dot(rows_x[...], jnp.concatenate([gate[...], up[...]], axis=1))
    act_gate = acts[:, :LANES]
    act_up = acts[:, LANES:]
    s = 1.0 / (1.0 + jnp.exp(-act_gate))
    silu = act_gate * s
    hidden[:, pl.ds(pl.multiple_of(step * LANES, LANES), LANES)] = (silu * act_up).astype(BF)
    by_gate[...] = act_up * s * (1.0 + act_gate * (1.0 - s))
    by_up[...] = silu

    @pl.when(step == pl.num_programs(0) - 1)
    def _():
        groups = parts.shape[0]
        for b in range(rows_x.shape[0] // BLOCK):
            out = dot(hidden[b * BLOCK : (b + 1) * BLOCK, :], down[...]).astype(BF)
            halves = jnp.concatenate(
                [
                    jnp.concatenate(
                        [
                            out[:, (2 * m + h) * LANES : (2 * m + h + 1) * LANES]
                            for m in range(groups)
                        ],
                        axis=1,
                    )
                    for h in range(2)
                ],
                axis=0,
            )
            packed = dot(perm_t[...], halves).astype(BF)
            for m in range(groups):
                parts[m, b * 2 * BLOCK : (b + 1) * 2 * BLOCK, :] = packed[
                    :, m * LANES : (m + 1) * LANES
                ]


def expert_forward(perm, perm_t, messages, w_gate, w_up, w_down):
    groups, sent, _ = messages.shape
    rows = sent // 2
    width, ff = w_gate.shape
    whole = lambda *shape: pl.BlockSpec(shape, lambda i: (0,) * len(shape))
    column = lambda n: pl.BlockSpec((n, LANES), lambda i: (0, i))
    return pl.pallas_call(
        forward_kernel,
        grid=(ff // LANES,),
        in_specs=[
            whole(*perm.shape),
            whole(*perm.shape),
            whole(*messages.shape),
            column(width),
            column(width),
            whole(ff, width),
        ],
        out_specs=[
            whole(rows, width),
            whole(rows, ff),
            column(rows),
            column(rows),
            whole(groups, sent, LANES),
        ],
        out_shape=[
            jax.ShapeDtypeStruct((rows, width), BF),
            jax.ShapeDtypeStruct((rows, ff), BF),
            jax.ShapeDtypeStruct((rows, ff), F32),
            jax.ShapeDtypeStruct((rows, ff), F32),
            jax.ShapeDtypeStruct((groups, sent, LANES), BF),
        ],
        compiler_params=params(),
        name="expert_forward",
    )(perm, perm_t, messages, w_gate, w_up, w_down)


def slot_masks(rows):
    source = iota((rows // CAP, rows), 1) // CAP == iota((rows // CAP, rows), 0)
    slot = iota((rows, LANES), 0) % CAP == iota((rows, LANES), 1)
    return source.astype(F32), slot.astype(F32)


def backward_kernel(
    perm, source, slot, msg, down, hidden, by_gate, by_up, rows_dy, d_gate, d_up, q_out
):
    unpack_rows(perm[...], msg, 0, rows_dy, rows_dy.shape[0] // BLOCK)
    grad_hidden = dot(rows_dy[...], down[...], ((1,), (1,)))
    d_gate[...] = (grad_hidden * by_gate[...]).astype(BF)
    d_up[...] = (grad_hidden * by_up[...]).astype(BF)
    q = row_sum(hidden[...].astype(F32) * grad_hidden)
    q_out[...] = dot(source[...], q * slot[...], precision=HIGHEST)


def expert_backward(perm, messages, w_down, hidden, by_gate, by_up):
    groups, sent, _ = messages.shape
    steps = 2
    rows = sent // 2
    part = rows // steps
    ff, width = w_down.shape
    source, slot = slot_masks(part)
    whole = lambda *shape: pl.BlockSpec(shape, lambda i: (0,) * len(shape))
    row = lambda n, m: pl.BlockSpec((n, m), lambda i: (i, 0))
    return pl.pallas_call(
        backward_kernel,
        grid=(steps,),
        in_specs=[
            whole(*perm.shape),
            whole(*source.shape),
            whole(*slot.shape),
            pl.BlockSpec((groups, sent // steps, LANES), lambda i: (0, i, 0)),
            whole(ff, width),
            row(part, ff),
            row(part, ff),
            row(part, ff),
        ],
        out_specs=[row(part, width), row(part, ff), row(part, ff), row(part // CAP, LANES)],
        out_shape=[
            jax.ShapeDtypeStruct((rows, width), BF),
            jax.ShapeDtypeStruct((rows, ff), BF),
            jax.ShapeDtypeStruct((rows, ff), BF),
            jax.ShapeDtypeStruct((rows // CAP, LANES), F32),
        ],
        compiler_params=params(),
        name="expert_backward",
    )(perm, source, slot, messages, w_down, hidden, by_gate, by_up)


def add_squares(total, grad, to):
    step = pl.program_id(0)
    squares = jnp.sum(grad * grad, axis=0, keepdims=True)

    @pl.when(step == 0)
    def _():
        total[...] = squares

    @pl.when(step > 0)
    def _():
        total[...] += squares

    @pl.when(step == pl.num_programs(0) - 1)
    def _():
        to[...] = jnp.broadcast_to(row_sum(total[...]), to.shape)


def grad_in_kernel(rows_x, d_gate, d_up, g_gate, g_up, s_gate, s_up, t_gate, t_up):
    across = rows_x[...].T
    for d, g, s, t in ((d_gate, g_gate, s_gate, t_gate), (d_up, g_up, s_up, t_up)):
        grad = dot(across, d[...])
        g[...] = grad
        add_squares(t, grad, s)


def grad_in(rows_x, d_gate, d_up):
    rows, width = rows_x.shape
    ff = d_gate.shape[1]
    chunk = 256
    whole = lambda *shape: pl.BlockSpec(shape, lambda i: (0,) * len(shape))
    return pl.pallas_call(
        grad_in_kernel,
        grid=(width // chunk,),
        in_specs=[pl.BlockSpec((rows, chunk), lambda i: (0, i)), whole(rows, ff), whole(rows, ff)],
        out_specs=[pl.BlockSpec((chunk, ff), lambda i: (i, 0))] * 2 + [whole(1, LANES)] * 2,
        out_shape=[jax.ShapeDtypeStruct((width, ff), F32)] * 2
        + [jax.ShapeDtypeStruct((1, LANES), F32)] * 2,
        scratch_shapes=[pltpu.VMEM((1, ff), F32)] * 2,
        compiler_params=params(),
        name="grad_in",
    )(rows_x, d_gate, d_up)


def grad_down_kernel(hidden, rows_dy, g_down, s_down, across, total):
    @pl.when(pl.program_id(0) == 0)
    def _():
        across[...] = hidden[...].T

    grad = dot(across[...], rows_dy[...])
    g_down[...] = grad
    add_squares(total, grad, s_down)


def grad_down(hidden, rows_dy):
    rows, ff = hidden.shape
    width = rows_dy.shape[1]
    chunk = 256
    whole = lambda *shape: pl.BlockSpec(shape, lambda i: (0,) * len(shape))
    return pl.pallas_call(
        grad_down_kernel,
        grid=(width // chunk,),
        in_specs=[whole(rows, ff), pl.BlockSpec((rows, chunk), lambda i: (0, i))],
        out_specs=[pl.BlockSpec((ff, chunk), lambda i: (0, i)), whole(1, LANES)],
        out_shape=[
            jax.ShapeDtypeStruct((ff, width), F32),
            jax.ShapeDtypeStruct((1, LANES), F32),
        ],
        scratch_shapes=[pltpu.VMEM((ff, rows), BF), pltpu.VMEM((1, chunk), F32)],
        compiler_params=params(),
        name="grad_down",
    )(hidden, rows_dy)


NET_ROWS = 32


def two_parts(x):
    high = x.astype(BF)
    return high, (x - high.astype(F32)).astype(BF)


def spread_kernel(coef, to):
    k = UNITS * NET_ROWS
    c = 8 * NET_ROWS
    same = iota((k, c), 0) % NET_ROWS == iota((k, c), 1) % NET_ROWS
    feature = iota((k, c), 1) // NET_ROWS
    value = jnp.zeros((k, c), F32)
    for part in range(3):
        a = coef[:, part : part + 1]
        high = a.astype(BF).astype(F32)
        low = a - high
        if part < 2:
            values = (high, low, high)
        else:
            values = (high, low)
        for i, v in enumerate(values):
            value = jnp.where(feature == part * 3 + i, v, value)
    to[...] = jnp.where(same, value, 0.0).astype(BF)


def spread_weights(mlp_in, weight_scale):
    coef = jnp.stack([mlp_in[0], mlp_in[2], mlp_in[1] * weight_scale], axis=1)
    coef = jnp.repeat(coef, NET_ROWS, axis=0)
    return pl.pallas_call(
        spread_kernel,
        out_shape=jax.ShapeDtypeStruct((UNITS * NET_ROWS, 8 * NET_ROWS), BF),
        compiler_params=params(),
        name="spread_weights",
    )(coef)


def step_kernel(scalars, rms, spread, grad, weight, out, *, rows):
    n = NET_ROWS
    height, width = grad.shape
    inverse = rms[0]
    constant = scalars[2, 0]

    def features(r, c, lanes):
        w = weight[pl.ds(r, n), c : c + lanes]
        f0 = grad[pl.ds(r, n), c : c + lanes] * inverse
        h0, l0 = two_parts(f0)
        h2, l2 = two_parts(jnp.tanh(f0))
        return jnp.concatenate([h0, h0, l0, h2, h2, l2, w, w], axis=0)

    def network(feats):
        y = dot(spread[...], feats)
        total = jnp.full((n, feats.shape[1]), constant, F32)
        for j in range(UNITS):
            total = total + scalars[1, j] * jnp.maximum(y[j * n : (j + 1) * n], scalars[0, j])
        return total.astype(BF)

    def body(i, carry):
        r = pl.multiple_of(i * rows, rows)
        for pair in range(0, rows, 2 * n):
            at = [r + pair, r + pair + n]
            whole = width // 256 * 256
            for c in range(0, whole, 256):
                for a in at:
                    out[pl.ds(a, n), c : c + 256] = network(features(a, c, 256))
            if whole < width:
                u = network(jnp.concatenate([features(a, whole, 128) for a in at], axis=1))
                for i, a in enumerate(at):
                    out[pl.ds(a, n), whole:width] = u[:, i * 128 : (i + 1) * 128]
        return carry

    lax.fori_loop(0, height // rows, body, 0)


def learned_step(grad, weight, rms, spread, scalars):
    height, width = grad.shape
    block = 128
    tile = pl.BlockSpec((block, width), lambda i: (i, 0))
    return pl.pallas_call(
        functools.partial(step_kernel, rows=128),
        grid=(height // block,),
        in_specs=[
            pl.BlockSpec(memory_space=pltpu.SMEM),
            pl.BlockSpec(memory_space=pltpu.SMEM),
            pl.BlockSpec(spread.shape, lambda i: (0, 0)),
            tile,
            tile,
        ],
        out_specs=tile,
        out_shape=jax.ShapeDtypeStruct((height, width), BF),
        compiler_params=params(),
        name="learned_step",
    )(scalars, rms, spread, grad, weight)


def mix_kernel(mp, aux, tok_cols, back, out):
    del mp
    n = aux.shape[0]
    rows = back.shape[0]
    lane = iota((n, rows), 1)
    for h in range(2):
        total = tok_cols[:, h * LANES : (h + 1) * LANES].astype(F32)
        for k in range(2):
            base = (aux[:, 4 + k : 5 + k] * (2 * CAP) + aux[:, 6 + k : 7 + k]).astype(jnp.int32)
            pick = (base + h * CAP == lane).astype(F32).astype(BF)
            total = total + aux[:, k : k + 1] * dot(pick, back[...])
        out[:, h * LANES : (h + 1) * LANES] = total.astype(BF)


def mix(mp_index, aux, tokens, back):
    n = tokens.shape[0]
    cols = 2 * LANES
    whole = lambda *shape: pl.BlockSpec(shape, lambda i, mp: (0,) * len(shape))
    return pl.pallas_call(
        mix_kernel,
        grid_spec=pltpu.PrefetchScalarGridSpec(
            num_scalar_prefetch=1,
            grid=(1,),
            in_specs=[
                whole(n, LANES),
                pl.BlockSpec((n, cols), lambda i, mp: (0, mp[0])),
                whole(*back.shape),
            ],
            out_specs=whole(n, cols),
        ),
        out_shape=jax.ShapeDtypeStruct((n, cols), BF),
        compiler_params=params(),
        name="mix",
    )(mp_index, aux, tokens, back)


def logit_kernel(aux, q, out):
    n = aux.shape[0]
    experts = q.shape[0]
    hits = []
    slots = []
    got = []
    for k in range(2):
        expert = aux[:, 4 + k : 5 + k].astype(jnp.int32)
        place = aux[:, 6 + k : 7 + k].astype(jnp.int32)
        hits.append((expert == iota((n, experts), 1)).astype(F32))
        slots.append((place == iota((n, LANES), 1)).astype(F32))
        got.append(row_sum(dot(hits[k], q[...], precision=HIGHEST) * slots[k]))
    both = got[0] + got[1]
    total = jnp.zeros((experts, LANES), F32)
    for k in range(2):
        grad = (got[k] - aux[:, k : k + 1] * both) * (1.0 - aux[:, 2 + k : 3 + k])
        total = total + dot(hits[k], slots[k] * grad, ((0,), (0,)), precision=HIGHEST)
    out[...] = total


def logit_grads(aux, q):
    return pl.pallas_call(
        logit_kernel,
        out_shape=jax.ShapeDtypeStruct(q.shape, F32),
        compiler_params=params(),
        name="logit_grads",
    )(aux, q)


def router_kernel(source, slot, grads, rows_x, out):
    column = row_sum(dot(source[...], grads[...], ((0,), (0,)), precision=HIGHEST) * slot[...])
    total = jnp.zeros((1, rows_x.shape[1]), F32)
    part = rows_x.shape[0] // 4
    for b in range(4):
        at = slice(b * part, (b + 1) * part)
        total = total + jnp.sum(rows_x[at, :].astype(F32) * column[at, :], axis=0, keepdims=True)
    out[...] = total


def router_column(grads, rows_x):
    source, slot = slot_masks(rows_x.shape[0])
    return pl.pallas_call(
        router_kernel,
        out_shape=jax.ShapeDtypeStruct((1, rows_x.shape[1]), F32),
        compiler_params=params(),
        name="router_column",
    )(source, slot, grads, rows_x)


def router_step_kernel(net, parts, weight, out):
    experts = weight.shape[0]
    grad = parts[0:experts, :]
    for m in range(1, parts.shape[0] // experts):
        grad = grad + parts[m * experts : (m + 1) * experts, :]
    mean = jnp.sum(row_sum(grad * grad), axis=0, keepdims=True) * (1.0 / grad.size)
    f0 = grad / jnp.sqrt(mean + EPSILON)
    f1 = weight[...].astype(F32) * D**0.5
    f2 = jnp.tanh(f0)
    total = jnp.zeros_like(f0)
    for j in range(UNITS):
        total = total + net[4, j] * jnp.maximum(
            net[0, j] * f0 + net[1, j] * f1 + net[2, j] * f2 + net[3, j], 0.0
        )
    out[...] = total.T.astype(BF)


def router_step(net, parts, weight):
    return pl.pallas_call(
        router_step_kernel,
        in_specs=[
            pl.BlockSpec(memory_space=pltpu.SMEM),
            pl.BlockSpec(memory_space=pltpu.VMEM),
            pl.BlockSpec(memory_space=pltpu.VMEM),
        ],
        out_shape=jax.ShapeDtypeStruct(weight.shape[::-1], BF),
        compiler_params=params(),
        name="router_step",
    )(net, parts, weight)


def to_experts(x, peers):
    sent = x.reshape(peers, x.shape[0] // peers, x.shape[1])
    return lax.all_to_all(sent, EXPERT, 0, 0, tiled=True).reshape(x.shape)


def on_device(
    tokens,
    cotangent,
    routes,
    router_weight,
    gate_weight,
    up_weight,
    down_weight,
    mlp_in,
    mlp_bias,
    mlp_out,
):
    experts = lax.axis_size(EXPERT)
    groups = lax.axis_size("mp")
    width = tokens.shape[1]
    mp_index = lax.axis_index("mp").astype(jnp.int32).reshape(1)
    w_gate = gate_weight[0]
    w_up = up_weight[0]
    w_down = down_weight[0]

    pos = jnp.arange(2 * BLOCK, dtype=jnp.int32)
    inner = pos % BLOCK
    source_row = inner + inner // CAP * CAP + pos // BLOCK * CAP
    perm = (source_row[:, None] == pos[None, :]).astype(BF)
    perm_t = (source_row[None, :] == pos[:, None]).astype(BF)
    spread_in = spread_weights(mlp_in, D**0.5)
    spread_down = spread_weights(mlp_in, FF**0.5)
    scalars = jnp.stack(
        [-mlp_bias, mlp_out, jnp.broadcast_to(jnp.sum(mlp_bias * mlp_out), mlp_out.shape)]
    )
    net = jnp.concatenate([mlp_in, mlp_bias[None], mlp_out[None]], axis=0)
    router_across = router_weight.T

    send_x, send_dy, aux = send_rows(tokens, cotangent, routes, router_weight, mp_index)
    msg_x = lax.all_gather(to_experts(send_x, experts), "mp")
    msg_dy = lax.all_gather(to_experts(send_dy, experts), "mp")

    rows_x, hidden, by_gate, by_up, parts = expert_forward(
        perm, perm_t, msg_x, w_gate, w_up, w_down
    )
    swapped = lax.all_to_all(parts, "mp", 0, 0, tiled=True)
    expert_out = jnp.sum(swapped.astype(F32), axis=0).astype(BF)
    back = to_experts(expert_out, experts)

    rows_dy, d_gate, d_up, q = expert_backward(perm, msg_dy, w_down, hidden, by_gate, by_up)
    q_back = lax.all_to_all(q, EXPERT, 0, 0, tiled=True)
    g_gate, g_up, s_gate, s_up = grad_in(rows_x, d_gate, d_up)
    g_down, s_down = grad_down(hidden, rows_dy)
    squares = lax.psum(jnp.stack([s_gate[0, 0], s_up[0, 0], s_down[0, 0]]), EXPERT_MP)
    total_count = experts * width * w_gate.shape[1] * groups
    inverse = 1.0 / jnp.sqrt(squares / total_count + EPSILON)

    lg = lax.all_to_all(logit_grads(aux, q_back), EXPERT, 0, 0, tiled=True)
    column = router_column(lg, rows_x)
    router_parts = lax.all_gather(column, MP_EXPERT, tiled=True)

    gate_update = learned_step(g_gate, w_gate, inverse[0:1], spread_in, scalars)
    up_update = learned_step(g_up, w_up, inverse[1:2], spread_in, scalars)
    down_update = learned_step(g_down, w_down, inverse[2:3], spread_down, scalars)
    mixed = mix(mp_index, aux, tokens, back)
    router_update = router_step(net, router_parts, router_across)
    return (mixed, gate_update[None], up_update[None], down_update[None], router_update)


def solution(mesh):
    torus = Mesh(
        mesh.devices.reshape(8, 4, 2, mesh.shape["mp"]), ("expert_0", "expert_1", "expert_2", "mp")
    )
    placed = (
        P(EXPERT, None),
        P(EXPERT, None),
        P(EXPERT, None),
        P(),
        P(EXPERT, None, "mp"),
        P(EXPERT, None, "mp"),
        P(EXPERT, "mp", None),
        P(),
        P(),
        P(),
    )
    return jax.shard_map(
        on_device,
        mesh=torus,
        in_specs=placed,
        out_specs=(
            P(EXPERT, "mp"),
            P(EXPERT, None, "mp"),
            P(EXPERT, None, "mp"),
            P(EXPERT, "mp", None),
            P(),
        ),
        check_vma=False,
    )
```

time: 491 us -> 325 us (0.66); the launches traced: 484 us -> 323 us
  other arithmetic: 234 us -> 6.47 us
  Pallas kernels: 0 us -> 75.8 us
  waiting for transfers between devices: 14.5 us -> 55.1 us
  matrix products: 37.7 us -> 0 us
  between operations: 36.9 us -> 14 us
  starting transfers between devices: 14.3 us -> 26.2 us
    broadcast_in_dim x3 -> x0, other arithmetic: 182 us -> none  [the longest x1 61.1 us: on_device(): learned_step(grad_up, w_up, D ** 0.5, up_rms, mlp_in, mlp_bias, mlp_out)]
    pallas_call x0 -> x14, Pallas kernels: none -> 75.8 us  [the longest x3 33.7 us: learned_step(): pl.pallas_call(functools.partial(step_kernel, rows=128), grid=(height //...]
    convert_element_type x8 -> x5, other arithmetic: 47 us -> 3.06 us  [the longest x4 2.89 us: slot_masks(): return (source.astype(F32), slot.astype(F32))]
    dot_general x12 -> x0, matrix products: 37.7 us -> none  [the longest x1 7.17 us: on_device(): jnp.einsum('sd,sf->df', rows_x, d_up, preferred_element_type=jnp.float32)]
    psum x4 -> x1, blocking collectives: 39.3 us -> 76.5 us  [on_device(): lax.psum(jnp.stack([s_gate[0, 0], s_up[0, 0], s_down[0, 0]]), EXPERT_MP)]
    all_to_all x1 -> x2, blocking collectives: 85.6 us -> 48.5 us  [to_experts(): return lax.all_to_all(sent, EXPERT, 0, 0, tiled=True).reshape(x.shape)]
    all_to_all x2 -> x4, waiting for transfers between devices: 10.5 us -> 36.9 us  [the longest x1 18.3 us: on_device(): swapped = lax.all_to_all(parts, 'mp', 0, 0, tiled=True)]
    all_gather x0 -> x3, waiting for transfers between devices: none -> 18.1 us  [the longest x1 16.2 us: on_device(): msg_dy = lax.all_gather(to_experts(send_dy, experts), 'mp')]
  transfers between devices with their start and end apart: 6 -> 7, of which waited for: 3 -> 5; matrix products, arithmetic and copies ran while one was open for 44% -> 2% of each run, Pallas kernels for 0% -> 19%
where the time goes in v1:
time: 325 us; the launch traced here: 323 us
  blocking collectives  125 us (38%)
  Pallas kernels  75.8 us (23%)
  waiting for transfers between devices  55.1 us (17%)
  starting transfers between devices  26.2 us (8%)
  local copies, waits for them, and re-layouts  20.9 us (6%)
  between operations  14 us (4%)
  other arithmetic  6.47 us (2%)
    psum x1, blocking collectives, on_device(): lax.psum(jnp.stack([s_gate[0, 0], s_up[0, 0], s_down[0, 0]]), EXPERT_MP)  76.5 us
    all_to_all x2, blocking collectives, to_experts(): return lax.all_to_all(sent, EXPERT, 0, 0, tiled=True).reshape(x.shape)  48.5 us
    pallas_call x3, Pallas kernels, learned_step(): pl.pallas_call(functools.partial(step_kernel, rows=128), grid=(height //...  33.7 us
    unnamed x56, local copies, waits for them, and re-layouts  19.4 us
    all_to_all x1, waiting for transfers between devices, on_device(): swapped = lax.all_to_all(parts, 'mp', 0, 0, tiled=True)  18.3 us
    all_gather x1, waiting for transfers between devices, on_device(): msg_dy = lax.all_gather(to_experts(send_dy, experts), 'mp')  16.2 us
    pallas_call x1, Pallas kernels, expert_forward(): pl.pallas_call(forward_kernel, grid=(ff // LANES,), in_specs=[whole(*perm...  13.7 us
    all_to_all x1, starting transfers between devices, on_device(): q_back = lax.all_to_all(q, EXPERT, 0, 0, tiled=True)  10.7 us
  transfers between devices with their start and end apart: 7, of which 5 were waited for; matrix products, arithmetic and copies ran while one was open for 2% of the time, Pallas kernels for 19%

profile of v1, /device:TPU:1, one launch (start us, length us, event | category | flops | bytes accessed | tf_op | source)
XLA Modules:
  0.0 323.5 jit_solution(15549895101385717567)
XLA Ops:
  11.2 2.2 send_rows.1
  14.1 27.9 %all_to_all.42 = bf16[64,24,128]{2,1,0:T(8,128)(2,1)} all-to-all(bf16[64,24,128]{2,1,0:T(8,128)(2,1)S(1)} %bitcast.59), channel_id=1, replica_groups=mesh['expert_0'=8,'expert_1'=4,'expert_2'=2,'mp'=4] {'expert_0','expert_..., dimensions={0} | all-to-all | bytes 786432 | tf_op jit(solution)/shard_map/all_to_all | solution.py:541
  42.1 20.6 %all_to_all.43 = bf16[64,24,128]{2,1,0:T(8,128)(2,1)} all-to-all(bf16[64,24,128]{2,1,0:T(8,128)(2,1)S(1)} %bitcast.58), channel_id=1, replica_groups=mesh['expert_0'=8,'expert_1'=4,'expert_2'=2,'mp'=4] {'expert_0','expert_..., dimensions={0} | all-to-all | bytes 786432 | tf_op jit(solution)/shard_map/all_to_all | solution.py:541
  64.3 1.3 fusion.2.slot
  65.8 1.9 all-gather.5.cloned.1.call-done.msg
  67.7 13.7 %expert_forward.1 = (bf16[768,1024]{1,0:T(8,128)(2,1)S(1)}, bf16[768,896]{1,0:T(8,128)(2,1)S(1)}, f32[768,896]{1,0:T(8,128)}, f32[768,896]{1,0:T(8,128)}, bf16[4,1536,128]{2,1,0:T(8,128)(2,1)S(1)}) custom-call(bf16[384,384]{1,0:T(8,128)(2,1)S(1)} %get-tuple-element.56.perm, bf16[384,384]{1,0:T(8,128)(2,1)S(1)} %get-tuple-element.55.perm_t, ...), custom_call_target="tpu_custom_call" | custom-call | tf_op jit(solution)/shard_map/expert_forward/pallas_call | solution.py:173
  81.4 1.1 copy-done.11
  82.5 16.2 %all-gather.7.cloned.1.call-done.msg = bf16[4,1536,128]{2,1,0:T(8,128)(2,1)} async-done(((bf16[1,1536,128]{2,1,0:T(8,128)(2,1)}), bf16[4,1536,128]{2,1,0:T(8,128)(2,1)}) %all-gather.7.cloned.1.call-update) | async-done | bytes 1572880 | tf_op jit(solution)/shard_map/all_gather | solution.py:579
  100.5 6.7 %expert_backward.1 = (bf16[768,1024]{1,0:T(8,128)(2,1)}, bf16[768,896]{1,0:T(8,128)(2,1)S(1)}, bf16[768,896]{1,0:T(8,128)(2,1)S(1)}, f32[64,128]{1,0:T(8,128)}) custom-call(bf16[384,384]{1,0:T(8,128)(2,1)S(1)} %get-tuple-element.56.perm, f32[32,384]{1,0:T(8,128)S(1)} %copy-done.22, f32[384,128]{1,0:T(8,128)S(1)} %copy-done.17, ...), custom_call_target="tpu_custom_call" | custom-call | tf_op jit(solution)/shard_map/expert_backward/pallas_call | solution.py:229
  108.3 1.1 copy-done.15
  109.4 10.7 %all-to-all-start.4 = ((f32[64,1,128]{2,1,0:T(1,128)}), f32[64,1,128]{2,1,0:T(1,128)S(1)}, u32[]{:S(2)}, u32[]{:S(2)}) async-start(f32[64,1,128]{2,1,0:T(1,128)} %bitcast.26), calls=%async_computation.4 | async-start | bytes 65536 | tf_op jit(solution)/shard_map/all_to_all | solution.py:589
  120.1 9.3 %all-to-all-done.4 = f32[64,1,128]{2,1,0:T(1,128)S(1)} async-done(((f32[64,1,128]{2,1,0:T(1,128)}), f32[64,1,128]{2,1,0:T(1,128)S(1)}, u32[]{:S(2)}, u32[]{:S(2)}) %all-to-all-start.4) | async-done | bytes 32800 | tf_op jit(solution)/shard_map/all_to_all | solution.py:589
  129.4 1.5 logit_grads.1
  131.0 4.7 %all-to-all-start.5 = ((f32[64,1,128]{2,1,0:T(1,128)}), f32[64,1,128]{2,1,0:T(1,128)S(1)}, u32[]{:S(2)}, u32[]{:S(2)}) async-start(f32[64,1,128]{2,1,0:T(1,128)} %bitcast.29), calls=%async_computation.5 | async-start | bytes 65536 | tf_op jit(solution)/shard_map/all_to_all | solution.py:596
  135.7 9.3 %all-to-all-done.5 = f32[64,1,128]{2,1,0:T(1,128)S(1)} async-done(((f32[64,1,128]{2,1,0:T(1,128)}), f32[64,1,128]{2,1,0:T(1,128)S(1)}, u32[]{:S(2)}, u32[]{:S(2)}) %all-to-all-start.5) | async-done | bytes 32800 | tf_op jit(solution)/shard_map/all_to_all | solution.py:596
  146.1 1.4 router_column.1
  147.5 4.4 %all-to-all-start.1 = ((bf16[4,1536,128]{2,1,0:T(8,128)(2,1)}), bf16[4,1536,128]{2,1,0:T(8,128)(2,1)}, u32[]{:S(2)}, u32[]{:S(2)}) async-start(bf16[4,1536,128]{2,1,0:T(8,128)(2,1)} %copy-done.11), calls=%async_computation.1 | async-start | bytes 3145728 | tf_op jit(solution)/shard_map/all_to_all | solution.py:584
  153.8 18.3 %all-to-all-done.1 = bf16[4,1536,128]{2,1,0:T(8,128)(2,1)} async-done(((bf16[4,1536,128]{2,1,0:T(8,128)(2,1)}), bf16[4,1536,128]{2,1,0:T(8,128)(2,1)}, u32[]{:S(2)}, u32[]{:S(2)}) %all-to-all-start.1) | async-done | bytes 1572896 | tf_op jit(solution)/shard_map/all_to_all | solution.py:584
  172.1 2.5 reduce_sum.21
  174.6 6.4 %all-to-all-start.2 = ((bf16[64,24,128]{2,1,0:T(8,128)(2,1)}), bf16[64,24,128]{2,1,0:T(8,128)(2,1)}, u32[]{:S(2)}, u32[]{:S(2)}) async-start(bf16[64,24,128]{2,1,0:T(8,128)(2,1)} %bitcast.70), calls=%async_computation.2 | async-start | bytes 786432 | tf_op jit(solution)/shard_map/all_to_all | solution.py:541
  181.1 1.4 copy-done.10
  182.5 4.3 %grad_down.1 = (f32[896,1024]{1,0:T(8,128)}, f32[1,128]{1,0:T(1,128)S(1)}) custom-call(bf16[768,896]{1,0:T(8,128)(2,1)S(1)} %get-tuple-element.28.hidden, bf16[768,1024]{1,0:T(8,128)(2,1)S(1)} %copy-done.10), custom_call_target="tpu_custom_call" | custom-call | tf_op jit(solution)/shard_map/grad_down/pallas_call | solution.py:312
  186.8 6.6 %grad_in.1 = (f32[1024,896]{1,0:T(8,128)}, f32[1024,896]{1,0:T(8,128)}, f32[1,128]{1,0:T(1,128)S(1)}, f32[1,128]{1,0:T(1,128)S(1)}) custom-call(bf16[768,1024]{1,0:T(8,128)(2,1)S(1)} %get-tuple-element.26.rows_x, bf16[768,896]{1,0:T(8,128)(2,1)S(1)} %copy-done.14, bf16[768,896]{1,0:T(8,128)(2,1)S(1)} %copy-done.16), custom_call_target="tpu_custom_call" | custom-call | tf_op jit(solution)/shard_map/grad_in/pallas_call | solution.py:284
  193.9 76.5 %psum.7 = f32[3]{0:T(128)S(1)} all-reduce(f32[3]{0:T(128)S(1)} %pad_maximum_fusion.4), channel_id=1, replica_groups=mesh['expert_0'=8,'expert_1'=4,'expert_2'=2,'mp'=4] {'expert_0','expert_..., use_global_device_ids=true, to_apply=%region_2.3 | all-reduce | flops 3 | bytes 24 | tf_op jit(solution)/shard_map/psum | solution.py:592
  271.0 2.0 copy-done.7
  274.0 11.3 %learned_step.3 = bf16[1024,896]{1,0:T(8,128)(2,1)} custom-call(f32[3,16]{1,0:T(4,128)S(1)} %maximum_maximum_fusion.scalars, f32[1]{0:T(128)} %get-tuple-element.61.rms, bf16[512,256]{1,0:T(8,128)(2,1)S(1)} %copy-done.9, f32[1024,896]{1,0:T(8,128)S(1)} %copy-done.7, bf16[1024,896]{1,0:T(8,128)(2,1)S(1)} %bitcast.51), custom_call_target="tpu_custom_call" | custom-call | tf_op jit(solution)/shard_map/learned_step/pallas_call | solution.py:406
  285.3 2.0 copy-done.6
  287.4 11.3 %learned_step.4 = bf16[1024,896]{1,0:T(8,128)(2,1)} custom-call(f32[3,16]{1,0:T(4,128)S(1)} %maximum_maximum_fusion.scalars, f32[1]{0:T(128)} %get-tuple-element.60.rms, bf16[512,256]{1,0:T(8,128)(2,1)S(1)} %copy-done.9, f32[1024,896]{1,0:T(8,128)S(1)} %copy-done.6, bf16[1024,896]{1,0:T(8,128)(2,1)S(1)} %bitcast.53), custom_call_target="tpu_custom_call" | custom-call | tf_op jit(solution)/shard_map/learned_step/pallas_call | solution.py:406
  298.7 11.1 %learned_step.5 = bf16[896,1024]{1,0:T(8,128)(2,1)} custom-call(f32[3,16]{1,0:T(4,128)S(1)} %maximum_maximum_fusion.scalars, f32[1]{0:T(128)} %get-tuple-element.59.rms, bf16[512,256]{1,0:T(8,128)(2,1)S(1)} %spread_weights.3.spread, f32[896,1024]{1,0:T(8,128)S(1)} %copy-done.5, bf16[896,1024]{1,0:T(8,128)(2,1)S(1)} %bitcast.49), custom_call_target="tpu_custom_call" | custom-call | tf_op jit(solution)/shard_map/learned_step/pallas_call | solution.py:406
  309.8 2.9 mix.1
  312.7 1.4 copy.29
  314.1 2.1 router_step.1
  (86 shorter events, 15.2 us)
Async XLA Ops:
  7.2 60.6 %all-gather.5.cloned.1.call-start = ((), (), s32[]{:S(2)}) async-start(), calls=%async_computation.6 | async-start | bytes 1966080 | tf_op jit(solution)/shard_map/all_gather | solution.py:578
  9.1 1.0 copy-start.3
  10.2 1.0 copy-start.18
  42.1 56.7 %all-gather.7.cloned.1.call-start = ((), (), s32[]{:S(2)}) async-start(), calls=%async_computation.7 | async-start | bytes 1966080 | tf_op jit(solution)/shard_map/all_gather | solution.py:579
  81.4 1.1 copy-start.11
  98.8 0.9 copy-start.17
  99.7 0.8 copy-start.22
  100.5 28.9 %copy-start.20 = (f32[256,128]{1,0:T(8,128)S(1)}, f32[256,128]{1,0:T(8,128)}, u32[]{:S(2)}) copy-start(f32[256,128]{1,0:T(8,128)} %copy-done.19) | copy-start | bytes 393220
  107.2 1.1 copy-start.13
  108.3 1.1 copy-start.15
  109.4 20.0 %all-to-all-start.4 = ((f32[64,1,128]{2,1,0:T(1,128)}), f32[64,1,128]{2,1,0:T(1,128)S(1)}, u32[]{:S(2)}, u32[]{:S(2)}) async-start(f32[64,1,128]{2,1,0:T(1,128)} %bitcast.26), calls=%async_computation.4 | async-start | bytes 65536 | tf_op jit(solution)/shard_map/all_to_all | solution.py:589
  131.0 14.1 %all-to-all-start.5 = ((f32[64,1,128]{2,1,0:T(1,128)}), f32[64,1,128]{2,1,0:T(1,128)S(1)}, u32[]{:S(2)}, u32[]{:S(2)}) async-start(f32[64,1,128]{2,1,0:T(1,128)} %bitcast.29), calls=%async_computation.5 | async-start | bytes 65536 | tf_op jit(solution)/shard_map/all_to_all | solution.py:596
  135.7 177.0 %all-gather.9.cloned.1.call-start = ((), (), s32[]{:S(2)}) async-start(), calls=%async_computation.8 | async-start | bytes 1052672 | tf_op jit(solution)/shard_map/all_gather | solution.py:598
  145.1 1.0 copy-start.12
  147.5 4.4 %copy-start.23 = (f32[3,16]{1,0:T(4,128)S(1)}, f32[3,16]{1,0:T(4,128)}, u32[]{:S(2)}) copy-start(f32[3,16]{1,0:T(4,128)} %param.17) | copy-start | bytes 580
  147.5 5.0 %copy-start.24 = (f32[16]{0:T(128)S(1)}, f32[16]{0:T(128)}, u32[]{:S(2)}) copy-start(f32[16]{0:T(128)} %param.19) | copy-start | bytes 196
  147.5 5.0 %copy-start.25 = (f32[16]{0:T(128)S(1)}, f32[16]{0:T(128)}, u32[]{:S(2)}) copy-start(f32[16]{0:T(128)} %param.18) | copy-start | bytes 196
  147.5 24.6 %all-to-all-start.1 = ((bf16[4,1536,128]{2,1,0:T(8,128)(2,1)}), bf16[4,1536,128]{2,1,0:T(8,128)(2,1)}, u32[]{:S(2)}, u32[]{:S(2)}) async-start(bf16[4,1536,128]{2,1,0:T(8,128)(2,1)} %copy-done.11), calls=%async_computation.1 | async-start | bytes 3145728 | tf_op jit(solution)/shard_map/all_to_all | solution.py:584
  152.4 34.4 %copy-start.8 = (bf16[512,256]{1,0:T(8,128)(2,1)}, bf16[512,256]{1,0:T(8,128)(2,1)S(1)}, u32[]{:S(2)}) copy-start(bf16[512,256]{1,0:T(8,128)(2,1)S(1)} %spread_weights.2.spread) | copy-start | bytes 786436
  174.6 135.2 %all-to-all-start.2 = ((bf16[64,24,128]{2,1,0:T(8,128)(2,1)}), bf16[64,24,128]{2,1,0:T(8,128)(2,1)}, u32[]{:S(2)}, u32[]{:S(2)}) async-start(bf16[64,24,128]{2,1,0:T(8,128)(2,1)} %bitcast.70), calls=%async_computation.2 | async-start | bytes 786432 | tf_op jit(solution)/shard_map/all_to_all | solution.py:541
  181.1 1.4 copy-start.10
  182.5 4.3 %copy-start.14 = (bf16[768,896]{1,0:T(8,128)(2,1)S(1)}, bf16[768,896]{1,0:T(8,128)(2,1)}, u32[]{:S(2)}) copy-start(bf16[768,896]{1,0:T(8,128)(2,1)} %copy-done.13) | copy-start | bytes 4128772
  182.5 4.3 %copy-start.16 = (bf16[768,896]{1,0:T(8,128)(2,1)S(1)}, bf16[768,896]{1,0:T(8,128)(2,1)}, u32[]{:S(2)}) copy-start(bf16[768,896]{1,0:T(8,128)(2,1)} %copy-done.15) | copy-start | bytes 4128772
  186.8 84.3 %copy-start.1 = (bf16[1,1024,896]{2,1,0:T(8,128)(2,1)S(1)}, bf16[1,1024,896]{2,1,0:T(8,128)(2,1)}, u32[]{:S(2)}) copy-start(bf16[1,1024,896]{2,1,0:T(8,128)(2,1)} %param.14) | copy-start | bytes 5505028
  271.0 2.0 copy-start.7
  273.1 0.9 copy-start.9
  274.0 11.3 %copy-start.2 = (bf16[1,1024,896]{2,1,0:T(8,128)(2,1)S(1)}, bf16[1,1024,896]{2,1,0:T(8,128)(2,1)}, u32[]{:S(2)}) copy-start(bf16[1,1024,896]{2,1,0:T(8,128)(2,1)} %param.15) | copy-start | bytes 5505028
  285.3 2.0 copy-start.6
  287.4 11.3 %copy-start = (bf16[1,896,1024]{2,1,0:T(8,128)(2,1)S(1)}, bf16[1,896,1024]{2,1,0:T(8,128)(2,1)}, u32[]{:S(2)}) copy-start(bf16[1,896,1024]{2,1,0:T(8,128)(2,1)} %param.16) | copy-start | bytes 5505028
  287.4 11.3 %copy-start.5 = (f32[896,1024]{1,0:T(8,128)S(1)}, f32[896,1024]{1,0:T(8,128)}, u32[]{:S(2)}) copy-start(f32[896,1024]{1,0:T(8,128)} %get-tuple-element.39.grad) | copy-start | bytes 11010052
  298.7 11.1 %copy-start.4 = (bf16[256,1024]{1,0:T(8,128)(2,1)S(1)}, bf16[256,1024]{1,0:T(8,128)(2,1)}, u32[]{:S(2)}) copy-start(bf16[256,1024]{1,0:T(8,128)(2,1)} %tok_cols.3) | copy-start | bytes 1572868
  309.8 4.3 %copy-start.21 = (bf16[1024,64]{0,1:T(8,128)(2,1)S(1)}, bf16[1024,64]{0,1:T(8,128)(2,1)}, u32[]{:S(2)}) copy-start(bf16[1024,64]{0,1:T(8,128)(2,1)} %param.13) | copy-start | bytes 393220
  (1 other events, 0.7 us)
Sparse Core Ops, SparseCore 0:
  42.2 25.5 all-gather.4
  69.5 29.1 all-gather.6
  147.6 102.4 all-gather.8
